TPU v7x, 128 devices: a whole 4x4x4 slice. The times are simulated.
128 devices in a mesh: dp: 4 (over y), seq: 32 (over z, x, core).
Axes of the slice: x: 4, y: 4, z: 4, core: 2. Of those that a mesh axis runs over, the one named last changes fastest.
Arguments:
- queries: bfloat16 [4, 8192, 1024], P('dp', 'seq'), may hold values from -7.5 to 7.5
- keys: bfloat16 [4, 8192, 1024], P('dp', 'seq'), may hold values from -7.5 to 7.5
- values: bfloat16 [4, 8192, 1024], P('dp', 'seq'), may hold values from -7.5 to 7.5
- grad_out: bfloat16 [4, 8192, 1024], P('dp', 'seq'), may hold values from -3 to 3
- w_out: bfloat16 [1024, 1024], replicated, may hold values from -0.1875 to 0.1875
Outputs:
- mixed: bfloat16 [4, 8192, 1024], P('dp', 'seq')
- grad_queries: bfloat16 [4, 8192, 1024], P('dp', 'seq')
- grad_keys: bfloat16 [4, 8192, 1024], P('dp', 'seq')
- grad_values: bfloat16 [4, 8192, 1024], P('dp', 'seq')
- grad_w_out: float32 [1024, 1024], P(('dp', 'seq'))
All inputs are finite; a program needn't handle non-finite values.
Results may differ from a plain program's by a relative error of at most 0.03.
Values may be sent and summed in bfloat16 or wider, within the bound.
A program may use at most 128 MiB of HBM per device.

v0:
```python
import math

import jax
import jax.numpy as jnp
from jax import lax
from jax.sharding import PartitionSpec as P

HEADS = 8
HEAD_DIM = 128
BLOCK = 128
LOCAL_LEVELS = 1


LOG_TWO = math.log(2.0)


def partner(block, axis, distance):
    count = lax.axis_size(axis)
    route = []
    for low in range(count):
        high = low | 1 << distance
        if high != low and high < count:
            route += [(low, high), (high, low)]
    return lax.ppermute(block, axis, route)


def pooled(rows):
    shape = rows.shape
    pairs = rows.astype(jnp.float32).reshape(shape[:-2] + (shape[-2] // 2, 2, shape[-1]))
    return ((pairs[..., 0, :] + pairs[..., 1, :]) * 0.5).astype(jnp.bfloat16)


def grouped(per_token, groups):
    return jnp.transpose(per_token.reshape(groups, -1, per_token.shape[-1]), (0, 2, 1))


def ungrouped(blocks):
    return jnp.transpose(blocks, (0, 2, 1)).reshape(-1, blocks.shape[1])


def level_scores(level, query_blocks, key_blocks):
    scale = 1.0 / math.sqrt(HEAD_DIM)
    scores = jnp.einsum(
        "gqhd,gkhd->ghqk", query_blocks, key_blocks, preferred_element_type=jnp.float32
    )
    return jnp.repeat(scores * scale + level * LOG_TWO, 2**level, axis=2)


def body(queries, keys, values, grad_out, w_out):
    seq_devices = lax.axis_size("seq")
    cross = seq_devices.bit_length() - 1
    levels = LOCAL_LEVELS + cross
    position = lax.axis_index("seq")
    scale = 1.0 / math.sqrt(HEAD_DIM)
    query_tok = queries[0]
    key_tok = keys[0]
    value_tok = values[0]
    grad_tok = grad_out[0]
    tokens = query_tok.shape[0]
    width = query_tok.shape[1]
    block = BLOCK
    query_pyramid = [query_tok]
    for level in range(1, levels):
        query_pyramid.append(pooled(query_pyramid[-1]))
    pair_pyramid = [jnp.stack([key_tok, value_tok])]
    level = 1
    pair_pyramid.append(pooled(pair_pyramid[-1]))
    summary = pair_pyramid[LOCAL_LEVELS]
    partners = []
    everyone = lax.all_gather(summary[None], "seq", axis=0, tiled=True)
    for bit in range(cross):
        start = (position >> bit ^ 1) << bit
        members = lax.dynamic_slice_in_dim(everyone, start, 2**bit, 0)
        members = jnp.transpose(members, (1, 0, 2, 3)).reshape(2, 2**bit * block, width)
        for repeat_number in range(bit):
            members = pooled(members)
        partners.append(members)

    def blocks_at(level):
        if level == 0:
            shape = (tokens // (2 * block), 2 * block, HEADS, HEAD_DIM)
            return (query_tok.reshape(shape), key_tok.reshape(shape), value_tok.reshape(shape))
        coarse = query_pyramid[level]
        remote = partners[level - LOCAL_LEVELS]
        shape = (1, block, HEADS, HEAD_DIM)
        return (
            coarse.reshape(1, coarse.shape[0], HEADS, HEAD_DIM),
            remote[0].reshape(shape),
            remote[1].reshape(shape),
        )

    scores_all = []
    top = None
    for level in range(levels):
        query_blocks, key_blocks, value_blocks = blocks_at(level)
        scores = level_scores(level, query_blocks, key_blocks)
        scores_all.append(scores)
        row_top = ungrouped(jnp.max(scores, axis=3))
        top = row_top if top is None else jnp.maximum(top, row_top)
    numer = jnp.zeros((tokens, HEADS, HEAD_DIM), jnp.float32)
    denom = jnp.zeros((tokens, HEADS), jnp.float32)
    for level in range(levels):
        query_blocks, key_blocks, value_blocks = blocks_at(level)
        groups = scores_all[level].shape[0]
        expo = jnp.exp(scores_all[level] - grouped(top, groups)[..., None])
        term = jnp.einsum(
            "ghrk,gkhd->grhd",
            expo.astype(jnp.bfloat16),
            value_blocks,
            preferred_element_type=jnp.float32,
        )
        numer = numer + term.reshape(tokens, HEADS, HEAD_DIM)
        denom = denom + ungrouped(jnp.sum(expo, axis=3))
    attended = (numer / denom[:, :, None]).reshape(tokens, width).astype(jnp.bfloat16)
    mixed = jnp.dot(attended, w_out, preferred_element_type=jnp.float32).astype(jnp.bfloat16)
    grad_att = jnp.einsum("se,de->sd", grad_tok, w_out, preferred_element_type=jnp.float32).astype(
        jnp.bfloat16
    )
    delta = jnp.einsum(
        "shd,shd->sh",
        grad_att.reshape(tokens, HEADS, HEAD_DIM),
        attended.reshape(tokens, HEADS, HEAD_DIM),
        preferred_element_type=jnp.float32,
    )
    query_grads = [jnp.zeros((tokens // 2**level, width), jnp.float32) for level in range(levels)]
    pair_grads = [
        jnp.zeros((2, tokens // 2**level, width), jnp.float32) for level in range(LOCAL_LEVELS + 1)
    ]
    partner_grads = []
    for level in range(levels):
        query_blocks, key_blocks, value_blocks = blocks_at(level)
        groups = scores_all[level].shape[0]
        prob = (
            jnp.exp(scores_all[level] - grouped(top, groups)[..., None])
            / grouped(denom, groups)[..., None]
        )
        grad_rows = grad_att.reshape(groups, -1, HEADS, HEAD_DIM)
        value_grad = jnp.einsum(
            "ghrk,grhd->gkhd",
            prob.astype(jnp.bfloat16),
            grad_rows,
            preferred_element_type=jnp.float32,
        )
        prob_grad = jnp.einsum(
            "grhd,gkhd->ghrk", grad_rows, value_blocks, preferred_element_type=jnp.float32
        )
        score_grad = prob * (prob_grad - grouped(delta, groups)[..., None])
        summed = (
            score_grad.reshape(groups, HEADS, -1, 2**level, score_grad.shape[3])
            .sum(axis=3)
            .astype(jnp.bfloat16)
        )
        query_grad = (
            jnp.einsum("ghqk,gkhd->gqhd", summed, key_blocks, preferred_element_type=jnp.float32)
            * scale
        )
        key_grad = (
            jnp.einsum("ghqk,gqhd->gkhd", summed, query_blocks, preferred_element_type=jnp.float32)
            * scale
        )
        query_grads[level] = query_grad.reshape(-1, width)
        if level == 0:
            pair_grads[0] = jnp.stack(
                [key_grad.reshape(tokens, width), value_grad.reshape(tokens, width)]
            )
        else:
            partner_grads.append(
                jnp.stack([key_grad.reshape(block, width), value_grad.reshape(block, width)])
            )
    upward = jnp.zeros((2, block, width), jnp.float32)
    for bit in reversed(range(cross)):
        spread = 0.5 * jnp.repeat(upward, 2, axis=1)
        upper = position >> bit & 1 == 1
        own_part = jnp.where(upper, spread[:, block:], spread[:, :block])
        their_part = jnp.where(upper, spread[:, :block], spread[:, block:])
        returned = partner(partner_grads[bit] + their_part, "seq", bit)
        upward = own_part + returned
    pair_grads[LOCAL_LEVELS] = upward
    for level in range(levels - 1, 0, -1):
        query_grads[level - 1] = query_grads[level - 1] + 0.5 * jnp.repeat(
            query_grads[level], 2, axis=0
        )
    level = 1
    pair_grads[level - 1] = pair_grads[level - 1] + 0.5 * jnp.repeat(pair_grads[level], 2, axis=1)
    all_tokens = queries.shape[0] * tokens * lax.axis_size("dp") * seq_devices
    factor = 1.0 / math.sqrt(all_tokens)
    weight_term = (
        jnp.einsum("sd,se->de", attended, grad_tok, preferred_element_type=jnp.float32) * factor
    )
    grad_w_out = lax.psum_scatter(weight_term, ("dp", "seq"), scatter_dimension=0, tiled=True)
    grad_queries = query_grads[0].astype(jnp.bfloat16)[None]
    grad_keys = pair_grads[0][0].astype(jnp.bfloat16)[None]
    grad_values = pair_grads[0][1].astype(jnp.bfloat16)[None]
    return (mixed[None], grad_queries, grad_keys, grad_values, grad_w_out)


def solution(mesh):
    placed = (
        P("dp", "seq", None),
        P("dp", "seq", None),
        P("dp", "seq", None),
        P("dp", "seq", None),
        P(),
    )
    return jax.shard_map(
        body,
        mesh=mesh,
        in_specs=placed,
        out_specs=(
            P("dp", "seq", None),
            P("dp", "seq", None),
            P("dp", "seq", None),
            P("dp", "seq", None),
            P(("dp", "seq"), None),
        ),
        check_vma=False,
    )
```

profile of v0, /device:TPU:1, one launch (start us, length us, event | category | flops | bytes accessed | tf_op | source)
XLA Modules:
  0.0 981.2 jit_solution(15692257069907862875)
XLA Ops:
  21.8 2.9 convert_reduce_fusion.1
  37.4 51.2 %all-gather.3.cloned.1.call-done = bf16[64,128,1,1024]{3,1,2,0:T(8,128)(2,1)} async-done(((bf16[2,128,1,1024]{3,1,2,0:T(8,128)(2,1)}), bf16[64,128,1,1024]{3,1,2,0:T(8,128)(2,1)}) %all-gather.3.cloned.1.call-update) | async-done | bytes 16777232 | tf_op jit(solution)/shard_map/all_gather | solution.py:70
  88.6 3.2 convert_bitcast_fusion.1
  91.8 8.6 copy.750
  100.4 4.2 fusion.5
  117.4 3.2 copy.744
  120.7 14.2 %fusion.11 = bf16[2,256,1,1024]{3,0,2,1:T(2,128)(2,1)S(1)} fusion(f32[2,256,2,1024]{3,0,2,1:T(2,128)S(1)} %bitcast.449), kind=kLoop, calls=%fused_computation.22 | loop fusion | flops 1572864 | bytes 5242880 | tf_op jit(solution)/shard_map/convert_element_type | solution.py:30
  150.8 11.3 %convert_bitcast_fusion = f32[2,16,128,1024]{3,2,0,1:T(8,128)} fusion(bf16[32,2,128,1024]{3,2,1,0:T(8,128)(2,1)} %bitcast.453, s32[]{:T(128)S(6)} %select_n.66), kind=kLoop, calls=%fused_computation | loop fusion | flops 4194304 | bytes 25165828 | tf_op jit(solution)/shard_map/convert_element_type | solution.py:29
  162.2 27.4 %copy.758 = f32[2,16,128,1024]{3,0,2,1:T(2,128)S(1)} copy(f32[2,16,128,1024]{3,2,0,1:T(8,128)} %convert_bitcast_fusion) | data formatting | bytes 33554432 | tf_op jit(solution)/shard_map/convert_element_type | solution.py:29
  189.6 9.3 fusion.1
  198.9 10.4 %bitcast_convert_fusion = f32[2,512,2,1024]{3,0,2,1:T(2,128)} fusion(bf16[2,512,2,1024]{3,0,2,1:T(2,128)(2,1)} %bitcast.448), kind=kLoop, calls=%fused_computation.11 | loop fusion | flops 2097152 | bytes 12582912 | tf_op jit(solution)/shard_map/convert_element_type | solution.py:29
  209.3 5.3 fusion.3
  309.4 3.1 fusion.17
  317.5 3.9 convolution_multiply_fusion
  354.0 11.7 %collective-permute-done.1 = f32[2,128,1024]{1,2,0:T(8,128)} collective-permute-done((f32[2,128,1024]{1,2,0:T(8,128)}, f32[2,128,1024]{1,2,0:T(8,128)}, u32[]{:S(2)}, u32[]{:S(2)}) %collective-permute-start.1) | collective-permute-done | bytes 1048608 | tf_op jit(solution)/shard_map/ppermute | solution.py:24
  381.6 2.7 collective-permute-start.2
  397.7 9.0 collective-permute-done.2
  429.6 3.0 fusion.81
  432.6 13.6 %collective-permute-done.3 = f32[2,128,1024]{1,2,0:T(8,128)} collective-permute-done((f32[2,128,1024]{1,2,0:T(8,128)}, f32[2,128,1024]{1,2,0:T(8,128)}, u32[]{:S(2)}, u32[]{:S(2)}) %collective-permute-start.3) | collective-permute-done | bytes 1048608 | tf_op jit(solution)/shard_map/ppermute | solution.py:24
  456.7 2.7 maximum_add_fusion.4
  459.4 3.1 collective-permute-start.4
  467.8 3.0 mul.451
  486.2 3.7 mul.480
  493.2 480.8 %reduce-scatter.2.cloned.1.call-done = f32[8,1024]{1,0:T(8,128)} async-done(((f32[1024,1024]{1,0:T(8,128)}), f32[8,1024]{1,0:T(8,128)}) %reduce-scatter.2.cloned.1.call-update) | async-done | bytes 32784 | tf_op jit(solution)/shard_map/reduce_scatter | solution.py:190
  (411 shorter events, 273.7 us)
Async XLA Ops:
  7.2 21.6 %copy-start = (bf16[1024,1024]{1,0:T(8,128)(2,1)S(1)}, bf16[1024,1024]{1,0:T(8,128)(2,1)}, u32[]{:S(2)}) copy-start(bf16[1024,1024]{1,0:T(8,128)(2,1)} %param.9) | copy-start | bytes 6291460
  7.2 81.4 %all-gather.3.cloned.1.call-start = ((), (), s32[]{:S(2)}) async-start(), calls=%async_computation.2 | async-start | bytes 17301504 | tf_op jit(solution)/shard_map/all_gather | solution.py:70
  12.1 961.8 %reduce-scatter.2.cloned.1.call-start = ((), (), s32[]{:S(2)}) async-start(), calls=%async_computation.1 | async-start | bytes 4227072 | tf_op jit(solution)/shard_map/reduce_scatter | solution.py:190
  16.2 212.5 %copy-start.33 = (bf16[128,1,1024]{0,2,1:T(8,128)(2,1)}, bf16[128,1,1024]{0,2,1:T(8,128)(2,1)S(1)}, u32[]{:S(2)}) copy-start(bf16[128,1,1024]{0,2,1:T(8,128)(2,1)S(1)} %copy.930) | copy-start | bytes 786436
  20.9 9.7 copy-start.71
  148.3 13.9 %copy-start.30 = (bf16[1,128,1,1024]{1,3,2,0:T(8,128)(2,1)}, bf16[1,128,1,1024]{1,3,2,0:T(8,128)(2,1)S(1)}, u32[]{:S(2)}) copy-start(bf16[1,128,1,1024]{1,3,2,0:T(8,128)(2,1)S(1)} %copy.739) | copy-start | bytes 786436
  224.1 12.1 %copy-start.28 = (bf16[1,128,1,1024]{1,3,2,0:T(8,128)(2,1)}, bf16[1,128,1,1024]{1,3,2,0:T(8,128)(2,1)S(1)}, u32[]{:S(2)}) copy-start(bf16[1,128,1,1024]{1,3,2,0:T(8,128)(2,1)S(1)} %copy.761) | copy-start | bytes 786436
  228.7 16.7 %copy-start.35 = (bf16[1,1,128,1024]{2,3,1,0:T(8,128)(2,1)}, bf16[1,1,128,1024]{2,3,1,0:T(8,128)(2,1)S(1)}, u32[]{:S(2)}) copy-start(bf16[1,1,128,1024]{2,3,1,0:T(8,128)(2,1)S(1)} %copy.731) | copy-start | bytes 786436
  237.8 10.7 %copy-start.50 = (f32[8,32,8]{0,2,1:T(8,128)S(1)}, f32[8,32,8]{0,2,1:T(8,128)}, u32[]{:S(2)}) copy-start(f32[8,32,8]{0,2,1:T(8,128)} %copy-done.49) | copy-start | bytes 24580
  245.4 9.8 %copy-start.51 = (f32[8,64,128]{2,1,0:T(8,128)S(1)}, f32[8,64,128]{2,1,0:T(8,128)}, u32[]{:S(2)}) copy-start(f32[8,64,128]{2,1,0:T(8,128)} %get-tuple-element.56) | copy-start | bytes 786436
  262.2 8.8 copy-start.47
  299.7 26.3 %collective-permute-start = (f32[2,128,1024]{1,2,0:T(8,128)}, f32[2,128,1024]{1,2,0:T(8,128)}, u32[]{:S(2)}, u32[]{:S(2)}) collective-permute-start(f32[2,128,1024]{1,2,0:T(8,128)} %pad_maximum_fusion), channel_id=1, source_target_pairs={{0,16},{16,0},{1,17},{17,1},{2,18},{18,2},{3,19},{19,3},{4,20},{20... | collective-permute-start | bytes 3145736 | tf_op jit(solution)/shard_map/ppermute | solution.py:24
  341.8 23.9 %collective-permute-start.1 = (f32[2,128,1024]{1,2,0:T(8,128)}, f32[2,128,1024]{1,2,0:T(8,128)}, u32[]{:S(2)}, u32[]{:S(2)}) collective-permute-start(f32[2,128,1024]{1,2,0:T(8,128)} %maximum_add_fusion.1), channel_id=1, source_target_pairs={{0,8},{8,0},{1,9},{9,1},{2,10},{10,2},{3,11},{11,3},{4,12},{12,4},... | collective-permute-start | bytes 3145736 | tf_op jit(solution)/shard_map/ppermute | solution.py:24
  352.2 13.4 %copy-start.8 = (f32[2,128,1024]{1,2,0:T(8,128)S(1)}, f32[2,128,1024]{1,2,0:T(8,128)}, u32[]{:S(2)}) copy-start(f32[2,128,1024]{1,2,0:T(8,128)} %copy.918) | copy-start | bytes 3145732
  352.2 13.4 %copy-start.9 = (f32[2,128,1024]{1,2,0:T(8,128)S(1)}, f32[2,128,1024]{1,2,0:T(8,128)}, u32[]{:S(2)}) copy-start(f32[2,128,1024]{1,2,0:T(8,128)} %copy.919) | copy-start | bytes 3145732
  381.6 25.1 %collective-permute-start.2 = (f32[2,128,1024]{1,2,0:T(8,128)}, f32[2,128,1024]{1,2,0:T(8,128)}, u32[]{:S(2)}, u32[]{:S(2)}) collective-permute-start(f32[2,128,1024]{1,2,0:T(8,128)} %maximum_add_fusion.2), channel_id=1, source_target_pairs={{0,4},{4,0},{1,5},{5,1},{2,6},{6,2},{3,7},{7,3},{8,12},{12,8},{9,1... | collective-permute-start | bytes 3145736 | tf_op jit(solution)/shard_map/ppermute | solution.py:24
  385.8 6.8 copy-start.31
  388.4 7.5 copy-start.76
  395.9 10.8 %copy-start.5 = (f32[2,128,1024]{1,2,0:T(8,128)S(1)}, f32[2,128,1024]{1,2,0:T(8,128)}, u32[]{:S(2)}) copy-start(f32[2,128,1024]{1,2,0:T(8,128)} %copy.920) | copy-start | bytes 3145732
  395.9 10.8 %copy-start.6 = (f32[2,128,1024]{1,2,0:T(8,128)S(1)}, f32[2,128,1024]{1,2,0:T(8,128)}, u32[]{:S(2)}) copy-start(f32[2,128,1024]{1,2,0:T(8,128)} %copy.921) | copy-start | bytes 3145732
  422.6 23.6 %collective-permute-start.3 = (f32[2,128,1024]{1,2,0:T(8,128)}, f32[2,128,1024]{1,2,0:T(8,128)}, u32[]{:S(2)}, u32[]{:S(2)}) collective-permute-start(f32[2,128,1024]{1,2,0:T(8,128)} %maximum_add_fusion.3), channel_id=1, source_target_pairs={{0,2},{2,0},{1,3},{3,1},{4,6},{6,4},{5,7},{7,5},{8,10},{10,8},{9,1... | collective-permute-start | bytes 3145736 | tf_op jit(solution)/shard_map/ppermute | solution.py:24
  429.6 16.6 %copy-start.3 = (f32[2,128,1024]{1,2,0:T(8,128)S(1)}, f32[2,128,1024]{1,2,0:T(8,128)}, u32[]{:S(2)}) copy-start(f32[2,128,1024]{1,2,0:T(8,128)} %copy.922) | copy-start | bytes 3145732
  429.6 16.6 %copy-start.4 = (f32[2,128,1024]{1,2,0:T(8,128)S(1)}, f32[2,128,1024]{1,2,0:T(8,128)}, u32[]{:S(2)}) copy-start(f32[2,128,1024]{1,2,0:T(8,128)} %copy.923) | copy-start | bytes 3145732
  459.4 20.6 %collective-permute-start.4 = (f32[2,128,1024]{1,2,0:T(8,128)}, f32[2,128,1024]{1,2,0:T(8,128)}, u32[]{:S(2)}, u32[]{:S(2)}) collective-permute-start(f32[2,128,1024]{1,2,0:T(8,128)} %maximum_add_fusion.4), channel_id=1, source_target_pairs={{0,1},{1,0},{2,3},{3,2},{4,5},{5,4},{6,7},{7,6},{8,9},{9,8},{10,11... | collective-permute-start | bytes 3145736 | tf_op jit(solution)/shard_map/ppermute | solution.py:24
  (71 other events, 237.4 us)
Sparse Core Ops, SparseCore 0:
  12.2 76.2 all-gather.2
  321.5 652.4 reduce-scatter.1
where the time goes:
time: 999 us; the launch traced here: 981 us
  waiting for transfers between devices  568 us (57%)
  local copies, waits for them, and re-layouts  187 us (19%)
  other arithmetic  138 us (14%)
  matrix products  60.7 us (6%)
  between operations  15.9 us (2%)
  starting transfers between devices  10.8 us (1%)
    reduce_scatter x1, waiting for transfers between devices, body(): lax.psum_scatter(weight_term, ('dp', 'seq'), scatter_dimension=0, tiled=T...  481 us
    all_gather x1, waiting for transfers between devices, body(): everyone = lax.all_gather(summary[None], 'seq', axis=0, tiled=True)  51.2 us
    convert_element_type x16, other arithmetic, pooled(): return ((pairs[..., 0, :] + pairs[..., 1, :]) * 0.5).astype(jnp.bfloat16)  46.9 us
    convert_element_type x9, local copies, waits for them, and re-layouts, pooled(): rows.astype(jnp.float32)  44.6 us
    convert_element_type x14, other arithmetic, pooled(): rows.astype(jnp.float32)  39.4 us
    ppermute x5, waiting for transfers between devices, partner(): return lax.ppermute(block, axis, route)  36.5 us
    unnamed x195, local copies, waits for them, and re-layouts  33 us
  transfers between devices with their start and end apart: 7, of which 6 were waited for; matrix products, arithmetic and copies ran while one was open for 17% of the time, Pallas kernels for 0%

commit v1 on v0

v1 whole, which is shorter than its diff:
```python
import math

import jax
import jax.numpy as jnp
from jax import lax
from jax.experimental import pallas as pl
from jax.experimental.pallas import tpu as pltpu
from jax.sharding import PartitionSpec as P

HEADS = 8
HD = 128
TOK = 256
D = 1024
ROWS = {1: 128, 2: 64, 3: 32, 4: 16, 5: 8}
SCALE = 1.0 / math.sqrt(HD)
LOG_TWO = math.log(2.0)
F32 = jnp.float32
BF16 = jnp.bfloat16
MESH = pl.DeviceIdType.MESH
CORE, X1, X3, Z1, Z3 = 1, 2, 6, 8, 24


def dot(a, b, ca=1, cb=0):
    return lax.dot_general(a, b, (((ca,), (cb,)), ((), ())), preferred_element_type=F32)


def twice(x):
    return jnp.concatenate([x, x], axis=0)


def fold(x):
    n = x.shape[0] // 2
    return x[:n] + x[n:]


def wide(x, lanes=HD):
    return jnp.broadcast_to(x, (x.shape[0], lanes))


SCRATCH = {
    "raw": ((4, TOK, D), BF16),
    "w": ((D, D), BF16),
    "perm": ((TOK, TOK), BF16),
    "back": ((TOK, TOK), BF16),
    "tok": ((4, TOK, D), BF16),
    "ga": ((TOK, D), BF16),
    "att": ((TOK, D), BF16),
    "own1": ((2, 128, D), BF16),
    "own2": ((2, 64, D), BF16),
    "own3": ((2, 32, D), BF16),
    "own4": ((2, 16, D), BF16),
    "own5": ((16, D), BF16),
    "q1": ((128, D), BF16),
    "q2": ((64, D), BF16),
    "q3": ((32, D), BF16),
    "q4": ((16, D), BF16),
    "q5": ((8, D), BF16),
    "sib1": ((2, 128, D), BF16),
    "sib2": ((2, 128, D), BF16),
    "sib3": ((2, 128, D), BF16),
    "sib4": ((2, 128, D), BF16),
    "land5": ((16, 16, D), BF16),
    "sib5": ((2, 128, D), BF16),
    "e0": ((HEADS, TOK, TOK), BF16),
    "n0": ((HEADS, TOK, HD), F32),
    "m0": ((HEADS, TOK, HD), F32),
    "d0": ((HEADS, TOK, HD), F32),
    "gam": ((HEADS, TOK, HD), F32),
    "del": ((HEADS, TOK, HD), F32),
    "kv0": ((2, TOK, D), F32),
    "fin": ((2, TOK, D), BF16),
    "dq": ((TOK, D), BF16),
    "out": ((4, TOK, D), BF16),
    "gown": ((D, 512), F32),
    "g0s": ((D, 512), BF16),
    "g0r": ((D, 512), BF16),
    "ga1s": ((4, 256, 256), BF16),
    "ga1r": ((3, 256, 256), BF16),
    "ga2s": ((4, 64, 256), BF16),
    "ga2r": ((3, 64, 256), BF16),
    "ga2f": ((4, 64, 256), F32),
    "gb1s": ((4, 4, 64, 256), BF16),
    "gb1r": ((3, 4, 64, 256), BF16),
    "gb2s": ((4, 64, 256), BF16),
    "gb2r": ((3, 64, 256), BF16),
    "gb2f": ((4, 64, 256), F32),
    "gc1s": ((4, 16, 512), BF16),
    "gc1r": ((3, 16, 512), BF16),
    "gc1f": ((4, 16, 512), F32),
    "gds": ((2, 8, 512), F32),
    "gdr": ((8, 512), F32),
    "gout": ((8, D), F32),
}
for _l, _n in ROWS.items():
    SCRATCH["e%d" % _l] = ((HEADS, _n, HD), F32)
    SCRATCH["n%d" % _l] = ((HEADS, _n, HD), F32)
    SCRATCH["m%d" % _l] = ((HEADS, _n, HD), F32)
    SCRATCH["d%d" % _l] = ((HEADS, _n, HD), F32)
    SCRATCH["g%d" % _l] = ((HEADS, _n, HD), F32)
    SCRATCH["t%d" % _l] = ((HEADS, _n, HD), F32)
    SCRATCH["dq%d" % _l] = ((_n, D), F32)
BACK = {
    1: ((CORE, 128),),
    2: ((CORE, 64), (X1, 64)),
    3: ((CORE, 64), (X1, 32), (X3, 32)),
    4: ((CORE, 64), (X3, 32), (X1, 16), (Z1, 16)),
    5: ((CORE, 64), (X3, 32), (X1, 16), (Z1, 8), (Z3, 8)),
}
for _l, _rounds in BACK.items():
    for _i, (_p, _n) in enumerate(_rounds):
        _shape = (_n // 8, 16, D) if _l == 5 else (2, _n, D)
        SCRATCH["bs%d_%d" % (_l, _i)] = (_shape, BF16)
        SCRATCH["br%d_%d" % (_l, _i)] = (_shape, BF16)
    if _l > 1:
        SCRATCH["acc%d" % _l] = ((8, 16, D) if _l == 5 else (2, 64, D), F32)
NAMES = list(SCRATCH)
COPIES = 80


def kernel(q_in, k_in, v_in, g_in, w_in, mixed_o, gq_o, gk_o, gv_o, gw_o, *scratch):
    s = dict(zip(NAMES, scratch[: len(NAMES)]))
    ssem, rsem, lsem = scratch[len(NAMES) :]
    dp = lax.axis_index("dp")
    me = lax.axis_index("seq")
    core = me % 2
    x_at = (me // 2) % 4
    z_at = me // 8

    def flipped(bits):
        out = me
        for bit in range(5):
            if bits >> bit & 1:
                out = out + (1 - 2 * ((me // 2**bit) % 2)) * 2**bit
        return out

    def flip2(at, k):
        out = at
        for bit in range(2):
            if k >> bit & 1:
                out = out + (1 - 2 * ((at // 2**bit) % 2)) * 2**bit
        return out

    peers = [(dp, flipped(b)) for b in (1, 2, 4, 6, 8, 16, 24)]
    peers += [(flip2(dp, k), me) for k in (1, 2, 3)]
    barrier = pltpu.get_barrier_semaphore()
    for peer in peers:
        pl.semaphore_signal(barrier, inc=1, device_id=peer, device_id_type=MESH)

    loads = []
    for i, src in enumerate((k_in, v_in, q_in, g_in)):
        loads.append(pltpu.make_async_copy(src, s["raw"].at[i], lsem.at[i]))
    loads.append(pltpu.make_async_copy(w_in, s["w"], lsem.at[4]))
    for load in loads:
        load.start()

    sent = []
    counter = [0]
    by_name = {}

    def send(name, src, dst, device):
        i = counter[0]
        counter[0] += 1
        copy = pltpu.make_async_remote_copy(
            src_ref=src,
            dst_ref=dst,
            send_sem=ssem.at[i],
            recv_sem=rsem.at[i],
            device_id=device,
            device_id_type=MESH,
        )
        copy.start()
        sent.append(copy)
        by_name[name] = copy

    def got(name):
        by_name[name].wait_recv()

    def to(bits):
        return (dp, flipped(bits))

    def source(p):
        r = p // 8
        rev = (r % 2) * 16 + (r // 2 % 2) * 8 + (r // 4 % 2) * 4 + (r // 8 % 2) * 2 + r // 16
        return (p % 8) * 32 + rev

    rows = lax.broadcasted_iota(jnp.int32, (TOK, TOK), 0)
    cols = lax.broadcasted_iota(jnp.int32, (TOK, TOK), 1)
    s["perm"][...] = (cols == source(rows)).astype(F32).astype(BF16)
    s["back"][...] = (rows == source(cols)).astype(F32).astype(BF16)

    def loop(n, f):
        def step(i, carry):
            f(i)
            return carry

        lax.fori_loop(0, n, step, 0)

    def at(i, width=HD):
        return pl.ds(pl.multiple_of(i * width, width), width)

    def reorder(i):
        def chunk(c):
            s["tok"][i, :, at(c, 256)] = dot(s["perm"][...], s["raw"][i, :, at(c, 256)]).astype(BF16)

        loop(4, chunk)

    def halves(x):
        return (fold(x.astype(F32)) * 0.5).astype(BF16)

    loads[0].wait()
    reorder(0)
    loads[1].wait()
    reorder(1)

    def pyramid(c):
        fives = []
        for i in range(2):
            x = s["tok"][i, :, at(c, 256)]
            for level in range(1, 5):
                x = halves(x)
                s["own%d" % level][i, :, at(c, 256)] = x
            fives.append(fold(x.astype(F32)) * 0.5)
        s["own5"][:, at(c, 256)] = jnp.concatenate(fives, axis=0).astype(BF16)

    loop(4, pyramid)
    pl.semaphore_wait(barrier, len(peers))
    send("f5z3", s["own5"], s["land5"].at[0], to(Z3))
    send("f4z1", s["own4"], s["sib4"].at[:, pl.ds(0, 16)], to(Z1))
    send("f3x3", s["own3"], s["sib3"].at[:, pl.ds(0, 32)], to(X3))
    send("f2x1", s["own2"], s["sib2"].at[:, pl.ds(0, 64)], to(X1))
    send("f1", s["own1"], s["sib1"], to(CORE))

    def relay(name, was, level, n, bits):
        got(was)
        if level == 5:
            g = n // 8
            send(name, s["land5"].at[pl.ds(0, g)], s["land5"].at[pl.ds(g, g)], to(bits))
        else:
            ref = s["sib%d" % level]
            send(name, ref.at[:, pl.ds(0, n)], ref.at[:, pl.ds(n, n)], to(bits))

    loads[2].wait()
    reorder(2)

    def q_pyramid(c):
        x = s["tok"][2, :, at(c, 256)]
        for level in range(1, 6):
            y = fold(x.astype(F32)) * 0.5
            x = y.astype(BF16)
            s["q%d" % level][:, at(c, 256)] = x

    loop(4, q_pyramid)
    loads[3].wait()
    reorder(3)
    relay("f5z1", "f5z3", 5, 8, Z1)
    relay("f4x1", "f4z1", 4, 16, X1)
    relay("f3x1", "f3x3", 3, 32, X1)
    loads[4].wait()

    def grad_att(c):
        s["ga"][:, at(c, 256)] = dot(s["tok"][3], s["w"][at(c, 256), :], 1, 1).astype(BF16)

    loop(4, grad_att)
    relay("f5x1", "f5z1", 5, 16, X1)
    relay("f2c", "f2x1", 2, 64, CORE)
    relay("f4x3", "f4x1", 4, 32, X3)

    def zero_forward(h):
        sc = dot(s["tok"][2, :, at(h)], s["tok"][0, :, at(h)], 1, 1) * SCALE
        m = jnp.max(sc, axis=1, keepdims=True)
        e = jnp.exp(sc - m)
        s["d0"][h] = wide(jnp.sum(e, axis=1, keepdims=True))
        s["m0"][h] = wide(m)
        eb = e.astype(BF16)
        s["e0"][h] = eb
        s["n0"][h] = dot(eb, s["tok"][1, :, at(h)])

    loop(4, zero_forward)
    relay("f3c", "f3x1", 3, 64, CORE)
    relay("f5x3", "f5x1", 5, 32, X3)
    loop(4, lambda h: zero_forward(h + 4))
    relay("f4c", "f4x3", 4, 64, CORE)

    def coarse_forward(level):
        def head(h):
            sc = dot(s["q%d" % level][:, at(h)], s["sib%d" % level][0, :, at(h)], 1, 1)
            sc = sc * SCALE + level * LOG_TWO
            m = jnp.max(sc, axis=1, keepdims=True)
            e = jnp.exp(sc - m)
            s["d%d" % level][h] = wide(jnp.sum(e, axis=1, keepdims=True))
            s["m%d" % level][h] = wide(m)
            s["e%d" % level][h] = e
            s["n%d" % level][h] = dot(e.astype(BF16), s["sib%d" % level][1, :, at(h)])

        loop(HEADS, head)

    got("f1")
    coarse_forward(1)
    relay("f5c", "f5x3", 5, 64, CORE)
    got("f2c")
    coarse_forward(2)
    got("f3c")
    coarse_forward(3)
    got("f4c")
    coarse_forward(4)
    got("f5c")

    def unpack5(h):
        x = s["land5"][:, :, at(h)].astype(F32)
        s["sib5"][0, :, at(h)] = x[:, :8].reshape(128, HD).astype(BF16)
        s["sib5"][1, :, at(h)] = x[:, 8:].reshape(128, HD).astype(BF16)

    loop(HEADS, unpack5)
    coarse_forward(5)

    def merge(h):
        c, num, den = s["m5"][h], s["n5"][h], s["d5"][h]
        a, b = {}, {}
        for level in (4, 3, 2, 1):
            m = s["m%d" % level][h]
            spread = twice(c)
            c = jnp.maximum(m, spread)
            a[level] = jnp.exp(m - c)
            b[level] = jnp.exp(spread - c)
            num = s["n%d" % level][h] * a[level] + twice(num) * b[level]
            den = s["d%d" % level][h] * a[level] + twice(den) * b[level]
        m = s["m0"][h]
        spread = twice(c)
        c = jnp.maximum(m, spread)
        a0 = jnp.exp(m - c)
        b0 = jnp.exp(spread - c)
        num = s["n0"][h] * a0 + twice(num) * b0
        den = s["d0"][h] * a0 + twice(den) * b0
        inv = 1.0 / den
        att = (num * inv).astype(BF16)
        s["att"][:, at(h)] = att
        ga = s["ga"][:, at(h)].astype(F32)
        delta = wide(jnp.sum(ga * att.astype(F32), axis=1, keepdims=True))
        s["gam"][h] = a0 * inv
        s["del"][h] = delta
        weight = b0 * inv
        grad = fold(weight * ga)
        diff = fold(weight * delta)
        for level in range(1, 6):
            if level < 5:
                s["g%d" % level][h] = grad * a[level]
                s["t%d" % level][h] = diff * a[level]
                grad = fold(grad * b[level])
                diff = fold(diff * b[level])
            else:
                s["g5"][h] = grad
                s["t5"][h] = diff

    loop(HEADS, merge)

    other = 1 - core

    def weight_other(h):
        cols = pl.ds(pl.multiple_of(other * 512, 512), 512)
        s["g0s"][at(h), :] = dot(s["att"][:, at(h)], s["tok"][3, :, cols], 0, 0).astype(BF16)

    loop(HEADS, weight_other)
    send("g0", s["g0s"], s["g0r"], to(CORE))

    def coarse_backward(level):
        def head(h):
            key, value = s["sib%d" % level][0, :, at(h)], s["sib%d" % level][1, :, at(h)]
            grad = s["g%d" % level][h].astype(BF16)
            e = s["e%d" % level][h]
            ds = e * (dot(grad, value, 1, 1) - s["t%d" % level][h])
            ds = ds.astype(BF16)
            s["dq%d" % level][:, at(h)] = dot(ds, key) * SCALE
            dk = dot(ds, s["q%d" % level][:, at(h)], 0, 0) * SCALE
            dv = dot(e.astype(BF16), grad, 0, 0)
            if level == 1:
                s["bs1_0"][0, :, at(h)] = dk.astype(BF16)
                s["bs1_0"][1, :, at(h)] = dv.astype(BF16)
            elif level < 5:
                for i, x in enumerate((dk, dv)):
                    s["acc%d" % level][i, :, at(h)] = x[:64]
                    s["bs%d_0" % level][i, :, at(h)] = x[64:].astype(BF16)
            else:
                pair = jnp.concatenate([dk.reshape(16, 8, HD), dv.reshape(16, 8, HD)], axis=1)
                s["acc5"][:, :, at(h)] = pair[:8]
                s["bs5_0"][:, :, at(h)] = pair[8:].astype(BF16)

        loop(HEADS, head)
        send("b%d_0" % level, s["bs%d_0" % level], s["br%d_0" % level], to(CORE))

    def back_step(level, i):
        got("b%d_%d" % (level, i - 1))
        rounds = BACK[level]
        bits, n = rounds[i]
        held = rounds[i - 1][1]
        acc, came, out = (s[x % level] for x in ("acc%d", "br%%d_%d" % (i - 1), "bs%%d_%d" % i))

        def chunk(c):
            if level == 5:
                total = acc[: held // 8, :, at(c, 256)] + came[:, :, at(c, 256)].astype(F32)
                keep = (held - n) // 8
                out[:, :, at(c, 256)] = total[keep:].astype(BF16)
                if keep:
                    acc[:keep, :, at(c, 256)] = total[:keep]
            else:
                keep = held - n
                for j in range(2):
                    total = acc[j, :held, at(c, 256)] + came[j, :, at(c, 256)].astype(F32)
                    out[j, :, at(c, 256)] = total[keep:].astype(BF16)
                    if keep:
                        acc[j, :keep, at(c, 256)] = total[:keep]

        loop(4, chunk)
        send("b%d_%d" % (level, i), out, s["br%d_%d" % (level, i)], to(bits))

    coarse_backward(2)

    def weight_own(h):
        cols = pl.ds(pl.multiple_of(core * 512, 512), 512)
        s["gown"][at(h), :] = dot(s["att"][:, at(h)], s["tok"][3, :, cols], 0, 0)

    loop(HEADS, weight_own)
    back_step(2, 1)
    got("g0")

    def weight_sum(j):
        x = s["gown"][at(j, 64), :] + s["g0r"][at(j, 64), :].astype(F32)
        s["gown"][at(j, 64), :] = x
        s["ga1s"][j // 4, pl.ds(pl.multiple_of((j % 4) * 64, 64), 64), :] = x[:, :256].astype(BF16)
        s["gb1s"][j // 4, j % 4] = x[:, 256:].astype(BF16)

    loop(16, weight_sum)
    y_dev = [(flip2(dp, k), me) for k in (1, 2, 3)]
    z_dev = [(dp, flipped(8 * k)) for k in (1, 2, 3)]
    x_dev = [(dp, flipped(2 * k)) for k in (1, 2, 3)]
    for k in (1, 2, 3):
        send("ga1_%d" % k, s["ga1s"].at[flip2(dp, k)], s["ga1r"].at[k - 1], y_dev[k - 1])
        send("gb1_%d" % k, s["gb1s"].at[:, flip2(z_at, k)], s["gb1r"].at[k - 1], z_dev[k - 1])

    coarse_backward(5)
    coarse_backward(4)
    back_step(5, 1)
    coarse_backward(3)
    back_step(4, 1)
    back_step(3, 1)
    coarse_backward(1)
    back_step(5, 2)
    back_step(4, 2)

    def zero_backward(h):
        e = s["e0"][h]
        q, ga = s["tok"][2, :, at(h)], s["ga"][:, at(h)]
        k, v = s["tok"][0, :, at(h)], s["tok"][1, :, at(h)]
        gam, delta = s["gam"][h], s["del"][h]
        both = jnp.concatenate([delta, delta], axis=1)
        ds = (e.astype(F32) * (dot(ga, v, 1, 1) - both)).astype(BF16)
        gq = (q.astype(F32) * gam).astype(BF16)
        gg = (ga.astype(F32) * gam).astype(BF16)
        s["kv0"][0, :, at(h)] = dot(ds, gq, 0, 0) * SCALE
        s["kv0"][1, :, at(h)] = dot(e, gg, 0, 0)
        up = s["dq5"][:, at(h)]
        for level in (4, 3, 2, 1):
            up = s["dq%d" % level][:, at(h)] + 0.5 * twice(up)
        dq = dot(ds, k) * gam * SCALE + 0.5 * twice(up)
        s["dq"][:, at(h)] = dq.astype(BF16)

    loop(4, zero_backward)
    back_step(3, 2)
    back_step(4, 3)
    back_step(5, 3)

    def weight_first():
        for k in (1, 2, 3):
            got("ga1_%d" % k)
            got("gb1_%d" % k)

        def chunk(j):
            r = pl.ds(pl.multiple_of(dp * 256 + j * 64, 64), 64)
            x = s["gown"][r, :256]
            for k in range(3):
                x = x + s["ga1r"][k, at(j, 64), :].astype(F32)
            s["ga2f"][j] = x
            s["ga2s"][j] = x.astype(BF16)
            r = pl.ds(pl.multiple_of(j * 256 + z_at * 64, 64), 64)
            x = s["gown"][r, 256:]
            for k in range(3):
                x = x + s["gb1r"][k, j].astype(F32)
            s["gb2f"][j] = x
            s["gb2s"][j] = x.astype(BF16)

        loop(4, chunk)
        for k in (1, 2, 3):
            send("ga2_%d" % k, s["ga2s"].at[flip2(z_at, k)], s["ga2r"].at[k - 1], z_dev[k - 1])
            send("gb2_%d" % k, s["gb2s"].at[flip2(dp, k)], s["gb2r"].at[k - 1], y_dev[k - 1])

    loop(2, lambda h: zero_backward(h + 4))
    weight_first()
    loop(2, lambda h: zero_backward(h + 6))
    back_step(5, 4)

    stores = []

    def store(i, out):
        copy = pltpu.make_async_copy(s["out"].at[i], out, lsem.at[5 + i])
        copy.start()
        stores.append(copy)

    def ordered(i, src):
        def chunk(c):
            s["out"][i, :, at(c, 256)] = dot(s["back"][...], src(c)).astype(BF16)

        loop(4, chunk)

    ordered(1, lambda c: s["dq"][:, at(c, 256)])
    store(1, gq_o)

    def weight_second():
        for k in (1, 2, 3):
            got("ga2_%d" % k)
            got("gb2_%d" % k)
        a = s["ga2f"][z_at]
        b = s["gb2f"][dp]
        for k in range(3):
            a = a + s["ga2r"][k].astype(F32)
            b = b + s["gb2r"][k].astype(F32)
        x = jnp.concatenate([a, b], axis=1).reshape(4, 16, 512)
        s["gc1f"][...] = x
        s["gc1s"][...] = x.astype(BF16)
        for k in (1, 2, 3):
            send("gc1_%d" % k, s["gc1s"].at[flip2(x_at, k)], s["gc1r"].at[k - 1], x_dev[k - 1])

    weight_second()
    ordered(0, lambda c: dot(s["att"][...], s["w"][:, at(c, 256)]).astype(BF16))
    store(0, mixed_o)

    for k in (1, 2, 3):
        got("gc1_%d" % k)
    x = s["gc1f"][x_at]
    for k in range(3):
        x = x + s["gc1r"][k].astype(F32)
    s["gds"][0] = x[:8]
    s["gds"][1] = x[8:]
    send("gd", s["gds"].at[other], s["gdr"], to(CORE))

    for level in range(1, 6):
        got("b%d_%d" % (level, len(BACK[level]) - 1))

    def finish(h):
        for i in range(2):
            up = s["br5_4"][0, :, at(h)].astype(F32)[8 * i : 8 * i + 8]
            for level in (4, 3, 2, 1):
                own = s["br%d_%d" % (level, len(BACK[level]) - 1)][i, :, at(h)]
                up = own.astype(F32) + 0.5 * twice(up)
            up = s["kv0"][i, :, at(h)] + 0.5 * twice(up)
            s["fin"][i, :, at(h)] = up.astype(BF16)

    loop(HEADS, finish)
    ordered(2, lambda c: s["fin"][0, :, at(c, 256)])
    store(2, gk_o)
    ordered(3, lambda c: s["fin"][1, :, at(c, 256)])
    store(3, gv_o)

    factor = 1.0 / math.sqrt(4 * 8192)
    got("gd")
    mine = s["gds"][core]
    s["gout"][:, pl.ds(pl.multiple_of(core * 512, 512), 512)] = mine * factor
    s["gout"][:, pl.ds(pl.multiple_of(other * 512, 512), 512)] = s["gdr"][...] * factor
    last = pltpu.make_async_copy(s["gout"], gw_o, lsem.at[9])
    last.start()
    for copy in sent:
        copy.wait_send()
    for copy in stores:
        copy.wait()
    last.wait()


def body(queries, keys, values, grad_out, w_out):
    shape = jax.ShapeDtypeStruct((TOK, D), BF16)
    outs = pl.pallas_call(
        kernel,
        out_shape=(shape, shape, shape, shape, jax.ShapeDtypeStruct((8, D), F32)),
        in_specs=[pl.BlockSpec(memory_space=pl.ANY)] * 5,
        out_specs=[pl.BlockSpec(memory_space=pl.ANY)] * 5,
        scratch_shapes=[pltpu.VMEM(*SCRATCH[name]) for name in NAMES]
        + [
            pltpu.SemaphoreType.DMA((COPIES,)),
            pltpu.SemaphoreType.DMA((COPIES,)),
            pltpu.SemaphoreType.DMA((10,)),
        ],
        compiler_params=pltpu.CompilerParams(
            collective_id=0, has_side_effects=True, vmem_limit_bytes=60 * 1024 * 1024
        ),
    )(queries[0], keys[0], values[0], grad_out[0], w_out)
    return tuple(out[None] for out in outs[:4]) + (outs[4],)


def solution(mesh):
    tokens = P("dp", "seq", None)
    return jax.shard_map(
        body,
        mesh=mesh,
        in_specs=(tokens, tokens, tokens, tokens, P()),
        out_specs=(tokens, tokens, tokens, tokens, P(("dp", "seq"), None)),
        check_vma=False,
    )
```

time: 999 us -> 83.6 us (0.08); the launches traced: 981 us -> 83.1 us
  waiting for transfers between devices: 568 us -> 0 us
  local copies, waits for them, and re-layouts: 187 us -> 6.03 us
  other arithmetic: 138 us -> 0 us
  Pallas kernels: 0 us -> 76.4 us
  matrix products: 60.7 us -> 0 us
  between operations: 15.9 us -> 0.67 us
  starting transfers between devices: 10.8 us -> 0 us
    reduce_scatter x1 -> x0, waiting for transfers between devices: 481 us -> none  [body(): lax.psum_scatter(weight_term, ('dp', 'seq'), scatter_dimension=0, tiled=T...]
    convert_element_type x32 -> x0, other arithmetic: 88.6 us -> none  [the longest x16 46.9 us: pooled(): return ((pairs[..., 0, :] + pairs[..., 1, :]) * 0.5).astype(jnp.bfloat16)]
    pallas_call x0 -> x1, Pallas kernels: none -> 76.4 us  [body(): pl.pallas_call(kernel, out_shape=(shape, shape, shape, shape, jax.ShapeDt...]
    dot_general x39 -> x0, matrix products: 60.7 us -> none  [the longest x6 12.8 us: body(): jnp.einsum('ghrk,grhd->gkhd', prob.astype(jnp.bfloat16), grad_rows, prefe...]
    all_gather x1 -> x0, waiting for transfers between devices: 51.2 us -> none  [body(): everyone = lax.all_gather(summary[None], 'seq', axis=0, tiled=True)]
    convert_element_type x10 -> x0, local copies, waits for them, and re-layouts: 44.8 us -> none  [the longest x9 44.6 us: pooled(): rows.astype(jnp.float32)]
    ppermute x5 -> x0, waiting for transfers between devices: 36.5 us -> none  [partner(): return lax.ppermute(block, axis, route)]
    mul x22 -> x0, local copies, waits for them, and re-layouts: 33.3 us -> none  [the longest x7 8.51 us: body(): 0.5 * jnp.repeat(query_grads[level], 2, axis=0)]
  transfers between devices with their start and end apart: 7 -> 0, of which waited for: 6 -> 0; matrix products, arithmetic and copies ran while one was open for 17% -> 0% of each run, Pallas kernels for 0% -> 0%
where the time goes in v1:
time: 83.6 us; the launch traced here: 83.1 us
  Pallas kernels  76.4 us (91%)
  local copies, waits for them, and re-layouts  6.03 us (7%)
    pallas_call x1, Pallas kernels, body(): pl.pallas_call(kernel, out_shape=(shape, shape, shape, shape, jax.ShapeDt...  76.4 us
    unnamed x11, local copies, waits for them, and re-layouts  6.03 us

profile of v1, /device:TPU:1, one launch (start us, length us, event | category | flops | bytes accessed | tf_op | source)
XLA Modules:
  0.0 83.1 jit_solution(13053271634406007932)
XLA Ops:
  0.6 76.4 %shard_map.92 = (bf16[256,1024]{1,0:T(8,128)(2,1)}, bf16[256,1024]{1,0:T(8,128)(2,1)}, bf16[256,1024]{1,0:T(8,128)(2,1)}, bf16[256,1024]{1,0:T(8,128)(2,1)}, f32[8,1024]{1,0:T(8,128)}) custom-call(bf16[256,1024]{1,0:T(8,128)(2,1)} %bitcast.12, bf16[256,1024]{1,0:T(8,128)(2,1)} %bitcast.13, bf16[256,1024]{1,0:T(8,128)(2,1)} %bitcast.14, ...), custom_call_target="tpu_custom_call" | custom-call | tf_op jit(solution)/shard_map/pallas_call | solution.py:578
  77.0 0.0 copy-start.1
  77.1 0.0 copy-start
  77.1 0.0 copy-start.2
  77.1 2.0 %copy.15 = bf16[1,256,1024]{2,1,0:T(8,128)(2,1)} copy(bf16[1,256,1024]{2,1,0:T(8,128)(2,1)} %bitcast.11) | data formatting | bytes 1048576
  79.0 1.9 %copy.16 = bf16[1,256,1024]{2,1,0:T(8,128)(2,1)} copy(bf16[1,256,1024]{2,1,0:T(8,128)(2,1)} %bitcast.10) | data formatting | bytes 1048576
  80.9 0.0 copy-done.1
  80.9 0.8 copy.17
  81.7 0.0 copy-done
  81.7 0.8 copy.18
  82.5 0.0 copy-done.2
  82.5 0.6 copy.19
Async XLA Ops:
  77.0 3.9 %copy-start.1 = (bf16[256,1024]{1,0:T(8,128)(2,1)S(1)}, bf16[256,1024]{1,0:T(8,128)(2,1)}, u32[]{:S(2)}) copy-start(bf16[256,1024]{1,0:T(8,128)(2,1)} %get-tuple-element.12) | copy-start | bytes 1572868
  77.1 4.6 %copy-start = (bf16[256,1024]{1,0:T(8,128)(2,1)S(1)}, bf16[256,1024]{1,0:T(8,128)(2,1)}, u32[]{:S(2)}) copy-start(bf16[256,1024]{1,0:T(8,128)(2,1)} %get-tuple-element.13) | copy-start | bytes 1572868
  77.1 5.4 %copy-start.2 = (f32[8,1024]{1,0:T(8,128)S(1)}, f32[8,1024]{1,0:T(8,128)}, u32[]{:S(2)}) copy-start(f32[8,1024]{1,0:T(8,128)} %get-tuple-element.24) | copy-start | bytes 98308

commit v2 on v1

--- a/solution.py
+++ b/solution.py
@@ -17,7 +17,7 @@
 F32 = jnp.float32
 BF16 = jnp.bfloat16
 MESH = pl.DeviceIdType.MESH
-CORE, X1, X3, Z1, Z3 = 1, 2, 6, 8, 24
+CORE, X1, X3, Z1, Z2, Z3 = 1, 2, 6, 8, 16, 24
 
 
 def dot(a, b, ca=1, cb=0):
@@ -41,7 +41,6 @@
     "raw": ((4, TOK, D), BF16),
     "w": ((D, D), BF16),
     "perm": ((TOK, TOK), BF16),
-    "back": ((TOK, TOK), BF16),
     "tok": ((4, TOK, D), BF16),
     "ga": ((TOK, D), BF16),
     "att": ((TOK, D), BF16),
@@ -70,7 +69,7 @@
     "kv0": ((2, TOK, D), F32),
     "fin": ((2, TOK, D), BF16),
     "dq": ((TOK, D), BF16),
-    "out": ((4, TOK, D), BF16),
+    "mixed": ((TOK, D), BF16),
     "gown": ((D, 512), F32),
     "g0s": ((D, 512), BF16),
     "g0r": ((D, 512), BF16),
@@ -92,19 +91,15 @@
     "gout": ((8, D), F32),
 }
 for _l, _n in ROWS.items():
-    SCRATCH["e%d" % _l] = ((HEADS, _n, HD), F32)
-    SCRATCH["n%d" % _l] = ((HEADS, _n, HD), F32)
-    SCRATCH["m%d" % _l] = ((HEADS, _n, HD), F32)
-    SCRATCH["d%d" % _l] = ((HEADS, _n, HD), F32)
-    SCRATCH["g%d" % _l] = ((HEADS, _n, HD), F32)
-    SCRATCH["t%d" % _l] = ((HEADS, _n, HD), F32)
+    for _c in "enmdgt":
+        SCRATCH["%s%d" % (_c, _l)] = ((HEADS * _n, HD), F32)
     SCRATCH["dq%d" % _l] = ((_n, D), F32)
 BACK = {
     1: ((CORE, 128),),
     2: ((CORE, 64), (X1, 64)),
     3: ((CORE, 64), (X1, 32), (X3, 32)),
     4: ((CORE, 64), (X3, 32), (X1, 16), (Z1, 16)),
-    5: ((CORE, 64), (X3, 32), (X1, 16), (Z1, 8), (Z3, 8)),
+    5: ((CORE, 64), (X3, 32), (X1, 16), (Z3, 8), (Z2, 8)),
 }
 for _l, _rounds in BACK.items():
     for _i, (_p, _n) in enumerate(_rounds):
@@ -117,7 +112,40 @@
 COPIES = 80
 
 
-def kernel(q_in, k_in, v_in, g_in, w_in, mixed_o, gq_o, gk_o, gv_o, gw_o, *scratch):
+def source(p):
+    r = p // 8
+    rev = (r % 2) * 16 + (r // 2 % 2) * 8 + (r // 4 % 2) * 4 + (r // 8 % 2) * 2 + r // 16
+    return (p % 8) * 32 + rev
+
+
+def reordering(axis):
+    at = lax.broadcasted_iota(jnp.int32, (TOK, TOK), axis)
+    token = lax.broadcasted_iota(jnp.int32, (TOK, TOK), 1 - axis)
+    return (token == source(at)).astype(F32).astype(BF16)
+
+
+def restore(rows_in, gw_in, mixed_o, gq_o, gk_o, gv_o, gw_o, held, out, gw, sem):
+    loads = [pltpu.make_async_copy(rows_in.at[i], held.at[i], sem.at[i]) for i in range(4)]
+    loads.append(pltpu.make_async_copy(gw_in, gw, sem.at[4]))
+    for load in loads:
+        load.start()
+    back = reordering(1)
+    stores = []
+    for i, target in enumerate((mixed_o, gq_o, gk_o, gv_o)):
+        loads[i].wait()
+        for c in range(4):
+            cols = pl.ds(c * 256, 256)
+            out[i, :, cols] = dot(back, held[i, :, cols]).astype(BF16)
+        stores.append(pltpu.make_async_copy(out.at[i], target, sem.at[5 + i]))
+        stores[-1].start()
+    loads[4].wait()
+    stores.append(pltpu.make_async_copy(gw, gw_o, sem.at[9]))
+    stores[-1].start()
+    for store in stores:
+        store.wait()
+
+
+def kernel(q_in, k_in, v_in, g_in, w_in, rows_o, gw_o, *scratch):
     s = dict(zip(NAMES, scratch[: len(NAMES)]))
     ssem, rsem, lsem = scratch[len(NAMES) :]
     dp = lax.axis_index("dp")
@@ -178,24 +206,15 @@
     def to(bits):
         return (dp, flipped(bits))
 
-    def source(p):
-        r = p // 8
-        rev = (r % 2) * 16 + (r // 2 % 2) * 8 + (r // 4 % 2) * 4 + (r // 8 % 2) * 2 + r // 16
-        return (p % 8) * 32 + rev
-
-    rows = lax.broadcasted_iota(jnp.int32, (TOK, TOK), 0)
-    cols = lax.broadcasted_iota(jnp.int32, (TOK, TOK), 1)
-    s["perm"][...] = (cols == source(rows)).astype(F32).astype(BF16)
-    s["back"][...] = (rows == source(cols)).astype(F32).astype(BF16)
+    s["perm"][...] = reordering(0)
 
     def loop(n, f):
-        def step(i, carry):
+        for i in range(n):
             f(i)
-            return carry
-
-        lax.fori_loop(0, n, step, 0)
 
     def at(i, width=HD):
+        if isinstance(i, int):
+            return pl.ds(i * width, width)
         return pl.ds(pl.multiple_of(i * width, width), width)
 
     def reorder(i):
@@ -225,6 +244,7 @@
     loop(4, pyramid)
     pl.semaphore_wait(barrier, len(peers))
     send("f5z3", s["own5"], s["land5"].at[0], to(Z3))
+    send("f5z2", s["own5"], s["land5"].at[1], to(Z2))
     send("f4z1", s["own4"], s["sib4"].at[:, pl.ds(0, 16)], to(Z1))
     send("f3x3", s["own3"], s["sib3"].at[:, pl.ds(0, 32)], to(X3))
     send("f2x1", s["own2"], s["sib2"].at[:, pl.ds(0, 64)], to(X1))
@@ -252,7 +272,6 @@
     loop(4, q_pyramid)
     loads[3].wait()
     reorder(3)
-    relay("f5z1", "f5z3", 5, 8, Z1)
     relay("f4x1", "f4z1", 4, 16, X1)
     relay("f3x1", "f3x3", 3, 32, X1)
     loads[4].wait()
@@ -261,7 +280,8 @@
         s["ga"][:, at(c, 256)] = dot(s["tok"][3], s["w"][at(c, 256), :], 1, 1).astype(BF16)
 
     loop(4, grad_att)
-    relay("f5x1", "f5z1", 5, 16, X1)
+    got("f5z2")
+    relay("f5x1", "f5z3", 5, 16, X1)
     relay("f2c", "f2x1", 2, 64, CORE)
     relay("f4x3", "f4x1", 4, 32, X3)
 
@@ -281,18 +301,25 @@
     loop(4, lambda h: zero_forward(h + 4))
     relay("f4c", "f4x3", 4, 64, CORE)
 
+    def groups(n):
+        size = HEADS if n < 128 else 4
+        return [range(h, h + size) for h in range(0, HEADS, size)]
+
     def coarse_forward(level):
-        def head(h):
-            sc = dot(s["q%d" % level][:, at(h)], s["sib%d" % level][0, :, at(h)], 1, 1)
-            sc = sc * SCALE + level * LOG_TWO
+        n = ROWS[level]
+        sib = s["sib%d" % level]
+        for heads in groups(n):
+            part = [dot(s["q%d" % level][:, at(h)], sib[0, :, at(h)], 1, 1) for h in heads]
+            sc = jnp.concatenate(part, axis=0) * SCALE + level * LOG_TWO
             m = jnp.max(sc, axis=1, keepdims=True)
             e = jnp.exp(sc - m)
-            s["d%d" % level][h] = wide(jnp.sum(e, axis=1, keepdims=True))
-            s["m%d" % level][h] = wide(m)
-            s["e%d" % level][h] = e
-            s["n%d" % level][h] = dot(e.astype(BF16), s["sib%d" % level][1, :, at(h)])
-
-        loop(HEADS, head)
+            rows = pl.ds(heads[0] * n, len(heads) * n)
+            s["e%d" % level][rows, :] = e
+            s["m%d" % level][rows, :] = wide(m)
+            s["d%d" % level][rows, :] = wide(jnp.sum(e, axis=1, keepdims=True))
+            for i, h in enumerate(heads):
+                eb = e[i * n : (i + 1) * n].astype(BF16)
+                s["n%d" % level][at(h, n), :] = dot(eb, sib[1, :, at(h)])
 
     got("f1")
     coarse_forward(1)
@@ -314,16 +341,16 @@
     coarse_forward(5)
 
     def merge(h):
-        c, num, den = s["m5"][h], s["n5"][h], s["d5"][h]
+        c, num, den = (s[name][at(h, 8), :] for name in ("m5", "n5", "d5"))
         a, b = {}, {}
         for level in (4, 3, 2, 1):
-            m = s["m%d" % level][h]
+            m = s["m%d" % level][at(h, ROWS[level]), :]
             spread = twice(c)
             c = jnp.maximum(m, spread)
             a[level] = jnp.exp(m - c)
             b[level] = jnp.exp(spread - c)
-            num = s["n%d" % level][h] * a[level] + twice(num) * b[level]
-            den = s["d%d" % level][h] * a[level] + twice(den) * b[level]
+            num = s["n%d" % level][at(h, ROWS[level]), :] * a[level] + twice(num) * b[level]
+            den = s["d%d" % level][at(h, ROWS[level]), :] * a[level] + twice(den) * b[level]
         m = s["m0"][h]
         spread = twice(c)
         c = jnp.maximum(m, spread)
@@ -343,13 +370,13 @@
         diff = fold(weight * delta)
         for level in range(1, 6):
             if level < 5:
-                s["g%d" % level][h] = grad * a[level]
-                s["t%d" % level][h] = diff * a[level]
+                s["g%d" % level][at(h, ROWS[level]), :] = grad * a[level]
+                s["t%d" % level][at(h, ROWS[level]), :] = diff * a[level]
                 grad = fold(grad * b[level])
                 diff = fold(diff * b[level])
             else:
-                s["g5"][h] = grad
-                s["t5"][h] = diff
+                s["g5"][at(h, 8), :] = grad
+                s["t5"][at(h, 8), :] = diff
 
     loop(HEADS, merge)
 
@@ -363,13 +390,11 @@
     send("g0", s["g0s"], s["g0r"], to(CORE))
 
     def coarse_backward(level):
-        def head(h):
-            key, value = s["sib%d" % level][0, :, at(h)], s["sib%d" % level][1, :, at(h)]
-            grad = s["g%d" % level][h].astype(BF16)
-            e = s["e%d" % level][h]
-            ds = e * (dot(grad, value, 1, 1) - s["t%d" % level][h])
-            ds = ds.astype(BF16)
-            s["dq%d" % level][:, at(h)] = dot(ds, key) * SCALE
+        n = ROWS[level]
+        sib = s["sib%d" % level]
+
+        def finish_head(h, e, ds, grad):
+            s["dq%d" % level][:, at(h)] = dot(ds, sib[0, :, at(h)]) * SCALE
             dk = dot(ds, s["q%d" % level][:, at(h)], 0, 0) * SCALE
             dv = dot(e.astype(BF16), grad, 0, 0)
             if level == 1:
@@ -384,13 +409,29 @@
                 s["acc5"][:, :, at(h)] = pair[:8]
                 s["bs5_0"][:, :, at(h)] = pair[8:].astype(BF16)
 
-        loop(HEADS, head)
+        for heads in groups(n):
+            grads = [s["g%d" % level][at(h, n), :].astype(BF16) for h in heads]
+            part = [dot(g, sib[1, :, at(h)], 1, 1) for g, h in zip(grads, heads)]
+            rows = pl.ds(heads[0] * n, len(heads) * n)
+            e = s["e%d" % level][rows, :]
+            ds = e * (jnp.concatenate(part, axis=0) - s["t%d" % level][rows, :])
+            for i, h in enumerate(heads):
+                mine = slice(i * n, (i + 1) * n)
+                finish_head(h, e[mine], ds[mine].astype(BF16), grads[i])
         send("b%d_0" % level, s["bs%d_0" % level], s["br%d_0" % level], to(CORE))
 
     def back_step(level, i):
         got("b%d_%d" % (level, i - 1))
         rounds = BACK[level]
         bits, n = rounds[i]
+        if level == 5 and i == 3:
+            for c in range(4):
+                total = s["acc5"][:2, :, at(c, 256)] + s["br5_2"][:, :, at(c, 256)].astype(F32)
+                s["bs5_3"][:, :, at(c, 256)] = total[:1].astype(BF16)
+                s["bs5_4"][:, :, at(c, 256)] = total[1:].astype(BF16)
+            send("b5_3", s["bs5_3"], s["br5_3"], to(Z3))
+            send("b5_4", s["bs5_4"], s["br5_4"], to(Z2))
+            return
         held = rounds[i - 1][1]
         acc, came, out = (s[x % level] for x in ("acc%d", "br%%d_%d" % (i - 1), "bs%%d_%d" % i))
 
@@ -425,7 +466,7 @@
     def weight_sum(j):
         x = s["gown"][at(j, 64), :] + s["g0r"][at(j, 64), :].astype(F32)
         s["gown"][at(j, 64), :] = x
-        s["ga1s"][j // 4, pl.ds(pl.multiple_of((j % 4) * 64, 64), 64), :] = x[:, :256].astype(BF16)
+        s["ga1s"][j // 4, at(j % 4, 64), :] = x[:, :256].astype(BF16)
         s["gb1s"][j // 4, j % 4] = x[:, 256:].astype(BF16)
 
     loop(16, weight_sum)
@@ -495,23 +536,15 @@
     loop(2, lambda h: zero_backward(h + 4))
     weight_first()
     loop(2, lambda h: zero_backward(h + 6))
-    back_step(5, 4)
 
     stores = []
 
-    def store(i, out):
-        copy = pltpu.make_async_copy(s["out"].at[i], out, lsem.at[5 + i])
+    def store(i, src):
+        copy = pltpu.make_async_copy(src, rows_o.at[i], lsem.at[5 + i])
         copy.start()
         stores.append(copy)
 
-    def ordered(i, src):
-        def chunk(c):
-            s["out"][i, :, at(c, 256)] = dot(s["back"][...], src(c)).astype(BF16)
-
-        loop(4, chunk)
-
-    ordered(1, lambda c: s["dq"][:, at(c, 256)])
-    store(1, gq_o)
+    store(1, s["dq"])
 
     def weight_second():
         for k in (1, 2, 3):
@@ -529,8 +562,12 @@
             send("gc1_%d" % k, s["gc1s"].at[flip2(x_at, k)], s["gc1r"].at[k - 1], x_dev[k - 1])
 
     weight_second()
-    ordered(0, lambda c: dot(s["att"][...], s["w"][:, at(c, 256)]).astype(BF16))
-    store(0, mixed_o)
+
+    def mix(c):
+        s["mixed"][:, at(c, 256)] = dot(s["att"][...], s["w"][:, at(c, 256)]).astype(BF16)
+
+    loop(4, mix)
+    store(0, s["mixed"])
 
     for k in (1, 2, 3):
         got("gc1_%d" % k)
@@ -543,10 +580,12 @@
 
     for level in range(1, 6):
         got("b%d_%d" % (level, len(BACK[level]) - 1))
+    got("b5_3")
 
     def finish(h):
         for i in range(2):
-            up = s["br5_4"][0, :, at(h)].astype(F32)[8 * i : 8 * i + 8]
+            up = s["br5_3"][0, :, at(h)].astype(F32) + s["br5_4"][0, :, at(h)].astype(F32)
+            up = up[8 * i : 8 * i + 8]
             for level in (4, 3, 2, 1):
                 own = s["br%d_%d" % (level, len(BACK[level]) - 1)][i, :, at(h)]
                 up = own.astype(F32) + 0.5 * twice(up)
@@ -554,10 +593,8 @@
             s["fin"][i, :, at(h)] = up.astype(BF16)
 
     loop(HEADS, finish)
-    ordered(2, lambda c: s["fin"][0, :, at(c, 256)])
-    store(2, gk_o)
-    ordered(3, lambda c: s["fin"][1, :, at(c, 256)])
-    store(3, gv_o)
+    store(2, s["fin"].at[0])
+    store(3, s["fin"].at[1])
 
     factor = 1.0 / math.sqrt(4 * 8192)
     got("gd")
@@ -574,12 +611,12 @@
 
 
 def body(queries, keys, values, grad_out, w_out):
-    shape = jax.ShapeDtypeStruct((TOK, D), BF16)
-    outs = pl.pallas_call(
+    weight = jax.ShapeDtypeStruct((8, D), F32)
+    rows, gw = pl.pallas_call(
         kernel,
-        out_shape=(shape, shape, shape, shape, jax.ShapeDtypeStruct((8, D), F32)),
+        out_shape=(jax.ShapeDtypeStruct((4, TOK, D), BF16), weight),
         in_specs=[pl.BlockSpec(memory_space=pl.ANY)] * 5,
-        out_specs=[pl.BlockSpec(memory_space=pl.ANY)] * 5,
+        out_specs=[pl.BlockSpec(memory_space=pl.ANY)] * 2,
         scratch_shapes=[pltpu.VMEM(*SCRATCH[name]) for name in NAMES]
         + [
             pltpu.SemaphoreType.DMA((COPIES,)),
@@ -590,6 +627,19 @@
             collective_id=0, has_side_effects=True, vmem_limit_bytes=60 * 1024 * 1024
         ),
     )(queries[0], keys[0], values[0], grad_out[0], w_out)
+    outs = pl.pallas_call(
+        restore,
+        out_shape=(jax.ShapeDtypeStruct((TOK, D), BF16),) * 4 + (weight,),
+        in_specs=[pl.BlockSpec(memory_space=pl.ANY)] * 2,
+        out_specs=[pl.BlockSpec(memory_space=pl.ANY)] * 5,
+        scratch_shapes=[
+            pltpu.VMEM((4, TOK, D), BF16),
+            pltpu.VMEM((4, TOK, D), BF16),
+            pltpu.VMEM((8, D), F32),
+            pltpu.SemaphoreType.DMA((10,)),
+        ],
+        compiler_params=pltpu.CompilerParams(vmem_limit_bytes=60 * 1024 * 1024),
+    )(rows, gw)
     return tuple(out[None] for out in outs[:4]) + (outs[4],)
 
 

time: 83.6 us -> 61.3 us (0.73)
  Pallas kernels: 76.4 us -> 60.3 us
  local copies, waits for them, and re-layouts: 6.03 us -> 0 us
    pallas_call x1 -> x2, Pallas kernels: 76.4 us -> 60.3 us  [the longest x1 57.2 us: body(): pl.pallas_call(kernel, out_shape=(jax.ShapeDtypeStruct((4, TOK, D), BF16)...]
    unnamed x11 -> x0, local copies, waits for them, and re-layouts: 6.03 us -> none
where the time goes in v2:
time: 61.3 us; the launch traced here: 61.1 us
  Pallas kernels  60.3 us (98%)
  between operations  0.8 us (1%)
    pallas_call x1, Pallas kernels, body(): pl.pallas_call(kernel, out_shape=(jax.ShapeDtypeStruct((4, TOK, D), BF16)...  57.2 us
    pallas_call x1, Pallas kernels, body(): pl.pallas_call(restore, out_shape=(jax.ShapeDtypeStruct((TOK, D), BF16),)...  3.15 us

profile of v2, /device:TPU:1, one launch (start us, length us, event | category | flops | bytes accessed | tf_op | source)
XLA Modules:
  0.0 61.1 jit_solution(15608790009124958341)
XLA Ops:
  0.6 57.2 %shard_map.92 = (bf16[4,256,1024]{2,1,0:T(8,128)(2,1)}, f32[8,1024]{1,0:T(8,128)}) custom-call(bf16[256,1024]{1,0:T(8,128)(2,1)} %bitcast.8, bf16[256,1024]{1,0:T(8,128)(2,1)} %bitcast.9, bf16[256,1024]{1,0:T(8,128)(2,1)} %bitcast.10, bf16[256,1024]{1,0:T(8,128)(2,1)} %bitcast.11, bf16[1024,1024]{1,0:T(8,128)(2,1)} %w_in.1), custom_call_target="tpu_custom_call" | custom-call | tf_op jit(solution)/shard_map/pallas_call | solution.py:615
  57.8 3.1 %shard_map.93 = (bf16[256,1024]{1,0:T(8,128)(2,1)}, bf16[256,1024]{1,0:T(8,128)(2,1)}, bf16[256,1024]{1,0:T(8,128)(2,1)}, bf16[256,1024]{1,0:T(8,128)(2,1)}, f32[8,1024]{1,0:T(8,128)}) custom-call(bf16[4,256,1024]{2,1,0:T(8,128)(2,1)} %get-tuple-element.12.rows_in, f32[8,1024]{1,0:T(8,128)} %get-tuple-element.13.gw_in), custom_call_target="tpu_custom_call" | custom-call | tf_op jit(solution)/shard_map/pallas_call | solution.py:630
